TPU v7x, 32 devices: a whole 2x2x4 slice. The times are simulated.
32 devices in a mesh: dom: 16 (over z, x, core), feat: 2 (over y).
Axes of the slice: x: 2, y: 2, z: 4, core: 2. Of those that a mesh axis runs over, the one named last changes fastest.
Arguments:
- features: bfloat16 [65536, 1024], P('dom', 'feat'), may hold values from -6 to 6
- w_self: bfloat16 [1024, 256], P('feat'), may hold values from -0.1875 to 0.1875
- w_neigh: bfloat16 [1024, 256], P('feat'), may hold values from -0.1875 to 0.1875
- hidden_bias: float32 [256], replicated, may hold values from -3 to 3
- edge_tiles: bfloat16 [16, 102, 128, 128], P('dom'), may hold values from 0 to 0.099609375
- tile_dst: int32 [16, 102], P('dom'), may hold values from 0 to 31, as said below
- tile_src: int32 [16, 102], P('dom'), may hold values from 0 to 47, as said below
- tile_count: int32 [16], P('dom'), may hold values from 12 to 102, as said below
- bound_rows: int32 [16, 256], P('dom'), may hold values from 0 to 4095, as said below
- send_pick: int32 [16, 16, 128], P('dom'), may hold values from 0 to 255, as said below
- cotangent: bfloat16 [65536, 256], P(('dom', 'feat')), may hold values from -0.0234375 to 0.0234375
Outputs:
- hidden: bfloat16 [65536, 256], P(('dom', 'feat'))
- grad_self: bfloat16 [1024, 256], P('feat')
- grad_neigh: bfloat16 [1024, 256], P('feat')
- grad_bias: float32 [256], replicated
Inputs may be any that keep to these rules, and one draw needn't show every extreme that they name: Within a partition the pairs (tile_dst, tile_src) of its 102 slots are distinct. `tile_src`: A source block below 32 is a row tile of the partition itself; block 32 + q is the block received from partition q. Slots from tile_count[p] on are unused. Some partition uses all 102 slots. `bound_rows`: distinct within each partition. Each list send_pick[p, q] has no repeats.
All inputs are finite; a program needn't handle non-finite values.
Results may differ from a plain program's by a relative error of at most 0.009.
The roundings to bfloat16 on the way count: a program that leaves them out, or rounds other values in their place, can miss the bound.
Values may be sent and summed in bfloat16 or wider, within the bound.
A program may use at most 128 MiB of HBM per device.

v0:
```python
import jax
import jax.numpy as jnp
from jax import lax
from jax.sharding import PartitionSpec as P

TILE = 128


def tile_sums(source, local_tiles, dest_list, source_list, live_count, dest_tiles):
    slice_width = source.shape[1]
    blocks = source.reshape(source.shape[0] // TILE, TILE, slice_width)
    picked = jnp.take(blocks, source_list, axis=0)
    products = jnp.einsum("etc,ecf->etf", local_tiles, picked, preferred_element_type=jnp.float32)
    slot_ids = jnp.arange(source_list.shape[0], dtype=jnp.int32)
    live_slots = (slot_ids < live_count).astype(jnp.float32)
    dest_ids = jnp.arange(dest_tiles, dtype=jnp.int32)[:, None]
    onehot = (dest_list[None, :] == dest_ids).astype(jnp.float32) * live_slots[None, :]
    summed = jnp.einsum("de,etf->dtf", onehot, products, precision=lax.Precision.HIGHEST)
    return summed.reshape(dest_tiles * TILE, slice_width).astype(jnp.bfloat16)


def body(
    features,
    w_self,
    w_neigh,
    hidden_bias,
    edge_tiles,
    tile_dst,
    tile_src,
    tile_count,
    bound_rows,
    send_pick,
    cotangent,
):
    part_count = lax.axis_size("dom")
    slice_width = features.shape[1]
    node_rows = features.shape[0]
    boundary = jnp.take(features, bound_rows[0], axis=0)
    everyone = lax.all_gather(boundary, "dom", axis=0, tiled=True)
    pick_lists = lax.all_to_all(send_pick, "dom", split_axis=1, concat_axis=0, tiled=True)
    offsets = (jnp.arange(part_count, dtype=jnp.int32) * boundary.shape[0])[:, None]
    wanted = (pick_lists[:, 0, :] + offsets).reshape(-1)
    received = jnp.take(everyone, wanted, axis=0)
    source = jnp.concatenate([features, received], 0)
    aggregated = tile_sums(
        source, edge_tiles[0], tile_dst[0], tile_src[0], tile_count[0], node_rows // TILE
    )
    stacked = jnp.concatenate([features, aggregated], 1)
    weights = jnp.concatenate([w_self, w_neigh], 0)
    row_block = stacked
    summed = lax.psum_scatter(
        jnp.dot(row_block, weights, preferred_element_type=jnp.float32),
        "feat",
        scatter_dimension=0,
        tiled=True,
    )
    preact = summed + hidden_bias
    hidden = jnp.maximum(preact, 0.0).astype(jnp.bfloat16)
    pre_grad = jnp.where(preact > 0.0, cotangent, jnp.zeros_like(cotangent))
    shard_rows = lax.all_gather(pre_grad, "feat", axis=0, tiled=True)
    row_block = stacked
    product = lax.dot_general(
        row_block, shard_rows, (((0,), (0,)), ((), ())), preferred_element_type=jnp.float32
    )
    all_grads = product
    bias_grad = jnp.sum(shard_rows.astype(jnp.float32), 0)
    all_grads, bias_grad = lax.psum((all_grads, bias_grad), "dom")
    grad_self = all_grads[:slice_width]
    grad_neigh = all_grads[slice_width:]
    return (hidden, grad_self.astype(jnp.bfloat16), grad_neigh.astype(jnp.bfloat16), bias_grad)


def solution(mesh):
    placed = (
        P("dom", "feat"),
        P("feat", None),
        P("feat", None),
        P(),
        P("dom", None, None, None),
        P("dom", None),
        P("dom", None),
        P("dom"),
        P("dom", None),
        P("dom", None, None),
        P(("dom", "feat"), None),
    )
    return jax.shard_map(
        body,
        mesh=mesh,
        in_specs=placed,
        out_specs=(P(("dom", "feat"), None), P("feat", None), P("feat", None), P()),
        check_vma=False,
    )
```

profile of v0, /device:TPU:0, one launch (start us, length us, event | category | flops | bytes accessed | tf_op | source)
XLA Modules:
  0.0 343.9 jit_solution(6246623295148714957)
XLA Ops:
  7.2 0.8 compare_select_fusion.3
  8.9 4.6 %gather_fusion = bf16[256,512]{1,0:T(8,128)(2,1)} fusion(bf16[4096,512]{1,0:T(8,128)(2,1)} %param.11, s32[1024]{0:T(1024)S(1)} %pad_clamp_fusion.1), kind=kCustom, calls=%fused_computation | custom fusion | bytes 525312 | tf_op jit(solution)/shard_map/jit(_take)/gather | solution.py:38
  13.5 1.8 broadcast_select_fusion.1
  15.3 7.4 %all-to-all-start = ((s32[1,16,128]{2,0,1:T(1,128)}), s32[1,16,128]{2,0,1:T(1,128)S(1)}, u32[]{:S(2)}, u32[]{:S(2)}) async-start(s32[1,16,128]{2,0,1:T(1,128)} %bitcast.45), calls=%async_computation | async-start | bytes 16384 | tf_op jit(solution)/shard_map/all_to_all | solution.py:40
  24.7 4.3 %all-to-all-done = s32[1,16,128]{2,0,1:T(1,128)S(1)} async-done(((s32[1,16,128]{2,0,1:T(1,128)}), s32[1,16,128]{2,0,1:T(1,128)S(1)}, u32[]{:S(2)}, u32[]{:S(2)}) %all-to-all-start) | async-done | bytes 8224 | tf_op jit(solution)/shard_map/all_to_all | solution.py:40
  29.2 39.3 %all-gather.3.cloned.1.call-done = bf16[4096,512]{1,0:T(8,128)(2,1)} async-done(((bf16[256,512]{1,0:T(8,128)(2,1)}), bf16[4096,512]{1,0:T(8,128)(2,1)}) %all-gather.3.cloned.1.call-update) | async-done | bytes 4194320 | tf_op jit(solution)/shard_map/all_gather | solution.py:39
  68.5 12.2 %gather_fusion.1 = bf16[2048,512]{1,0:T(8,128)(2,1)} fusion(bf16[4096,512]{1,0:T(8,128)(2,1)} %all-gather.3.cloned.1.call-done, s32[2048]{0:T(1024)S(1)} %broadcast_clamp_fusion), kind=kCustom, calls=%fused_computation.1 | custom fusion | bytes 4202496 | tf_op jit(solution)/shard_map/jit(_take)/gather | solution.py:43
  80.7 1.9 broadcast_select_fusion
  82.6 0.9 copy-done.2
  83.5 3.0 pad_maximum_fusion.1
  86.5 10.2 %gather_fusion.2 = bf16[102,128,512]{2,1,0:T(8,128)(2,1)} fusion(bf16[48,128,512]{2,1,0:T(8,128)(2,1)} %bitcast.39, s32[1024]{0:T(1024)S(1)} %pad_clamp_fusion), kind=kCustom, calls=%fused_computation.2 | custom fusion | bytes 26739096 | tf_op jit(solution)/shard_map/jit(_take)/gather | solution.py:12
  96.7 13.8 %fusion.3 = f32[102,128,512]{1,2,0:T(8,128)} fusion(bf16[102,128,512]{2,1,0:T(8,128)(2,1)} %gather_fusion.2, pred[102]{0:T(512)(128)(4,1)S(1)} %compare_and_fusion.2, bf16[1,102,128,128]{3,2,1,0:T(8,128)(2,1)S(1)} %copy-done), kind=kOutput, calls=%fused_computation.6 | convolution fusion | flops 1717960704 | bytes 43450472 | tf_op jit(solution)/shard_map/etc,ecf->etf/dot_general | solution.py:13
  110.5 28.4 %copy.21 = f32[102,128,512]{2,0,1:T(8,128)} copy(f32[102,128,512]{1,2,0:T(8,128)} %fusion.3) | data formatting | bytes 53477376 | tf_op jit(solution)/shard_map/etc,ecf->etf/dot_general | solution.py:13
  139.0 16.6 %convolution_convert_fusion = bf16[32,128,512]{2,0,1:T(8,128)(2,1)S(1)} fusion(f32[102,128,512]{2,0,1:T(8,128)} %copy.21, f32[102]{0:T(128)S(1)} %compare_convert_fusion, s32[102]{0:T(128)S(1)} %bitcast.48), kind=kOutput, calls=%fused_computation.14 | convolution fusion | flops 2569017856 | bytes 30933808 | tf_op jit(solution)/shard_map/de,etf->dtf/dot_general | solution.py:18
  155.6 2.4 copy.22
  158.0 2.0 copy-done.5
  159.9 3.9 %fusion.8 = f32[4096,256]{1,0:T(8,128)} fusion(bf16[4096,512]{1,0:T(8,128)(2,1)S(1)} %bitcast.40, bf16[4096,512]{1,0:T(8,128)(2,1)S(1)} %copy-done.3, bf16[512,256]{1,0:T(8,128)(2,1)S(1)} %copy-done.10, bf16[512,256]{1,0:T(8,128)(2,1)S(1)} %copy-done.11), kind=kOutput, calls=%fused_computation.11 | convolution fusion | flops 2165309440 | bytes 13107200 | tf_op jit(solution)/shard_map/dot_general | solution.py:52
  164.1 52.8 %reduce-scatter.2.cloned.1.call-done = f32[2048,256]{1,0:T(8,128)} async-done(((f32[4096,256]{1,0:T(8,128)}), f32[2048,256]{1,0:T(8,128)}) %reduce-scatter.2.cloned.1.call-update) | async-done | bytes 2097168 | tf_op jit(solution)/shard_map/reduce_scatter | solution.py:51
  216.9 3.0 compare_select_fusion
  220.0 1.2 maximum_convert_fusion
  221.2 32.1 %all-gather.5.cloned.1.call-done = bf16[4096,256]{1,0:T(8,128)(2,1)} async-done(((bf16[2048,256]{1,0:T(8,128)(2,1)}), bf16[4096,256]{1,0:T(8,128)(2,1)}) %all-gather.5.cloned.1.call-update) | async-done | bytes 2097168 | tf_op jit(solution)/shard_map/all_gather | solution.py:60
  253.3 7.6 %fusion.7 = f32[1024,256]{1,0:T(8,128)} fusion(bf16[4096,256]{1,0:T(8,128)(2,1)} %all-gather.5.cloned.1.call-done, bf16[4096,512]{1,0:T(8,128)(2,1)} %bitcast.41, bf16[4096,512]{1,0:T(8,128)(2,1)} %param.11), kind=kOutput, calls=%fused_computation.10 | convolution fusion | flops 2164260864 | bytes 11534336 | tf_op jit(solution)/shard_map/dot_general | solution.py:62
  261.4 74.1 %all-reduce.2 = (bf16[1024,256]{1,0:T(8,128)(2,1)}, f32[256]{0:T(256)}) all-reduce(f32[1024,256]{1,0:T(8,128)} %fusion.7, f32[256]{0:T(256)S(1)} %convert_reduce_fusion), channel_id=1, replica_groups=mesh['dom'=16,'feat'=2] {'dom'}, use_global_device_ids=true, to_apply=%region_1.2 | all-reduce | flops 262400 | bytes 1574912 | tf_op jit(solution)/shard_map/psum | solution.py:67
  335.5 1.9 fusion.23
  (40 shorter events, 3.3 us)
Async XLA Ops:
  7.2 89.6 %copy-start = (bf16[1,102,128,128]{3,2,1,0:T(8,128)(2,1)S(1)}, bf16[1,102,128,128]{3,2,1,0:T(8,128)(2,1)}, u32[]{:S(2)}) copy-start(bf16[1,102,128,128]{3,2,1,0:T(8,128)(2,1)} %param.15) | copy-start | bytes 10027012
  7.2 61.4 %all-gather.3.cloned.1.call-start = ((), (), s32[]{:S(2)}) async-start(), calls=%async_computation.2 | async-start | bytes 4456448 | tf_op jit(solution)/shard_map/all_gather | solution.py:39
  15.3 13.8 %all-to-all-start = ((s32[1,16,128]{2,0,1:T(1,128)}), s32[1,16,128]{2,0,1:T(1,128)S(1)}, u32[]{:S(2)}, u32[]{:S(2)}) async-start(s32[1,16,128]{2,0,1:T(1,128)} %bitcast.45), calls=%async_computation | async-start | bytes 16384 | tf_op jit(solution)/shard_map/all_to_all | solution.py:40
  22.7 194.2 %reduce-scatter.2.cloned.1.call-start = ((), (), s32[]{:S(2)}) async-start(), calls=%async_computation.3 | async-start | bytes 6291456 | tf_op jit(solution)/shard_map/reduce_scatter | solution.py:51
  80.7 2.8 copy-start.2
  110.5 28.4 %copy-start.9 = (s32[1,102]{1,0:T(1,128)S(1)}, s32[1,102]{1,0:T(1,128)}, u32[]{:S(2)}) copy-start(s32[1,102]{1,0:T(1,128)} %param.16) | copy-start | bytes 1228
  155.5 4.4 %copy-start.3 = (bf16[4096,512]{1,0:T(8,128)(2,1)S(1)}, bf16[4096,512]{1,0:T(8,128)(2,1)}, u32[]{:S(2)}) copy-start(bf16[4096,512]{1,0:T(8,128)(2,1)} %param.11) | copy-start | bytes 12582916
  155.5 4.4 %copy-start.10 = (bf16[512,256]{1,0:T(8,128)(2,1)S(1)}, bf16[512,256]{1,0:T(8,128)(2,1)}, u32[]{:S(2)}) copy-start(bf16[512,256]{1,0:T(8,128)(2,1)} %param.13) | copy-start | bytes 786436
  155.6 4.4 %copy-start.11 = (bf16[512,256]{1,0:T(8,128)(2,1)S(1)}, bf16[512,256]{1,0:T(8,128)(2,1)}, u32[]{:S(2)}) copy-start(bf16[512,256]{1,0:T(8,128)(2,1)} %param.12) | copy-start | bytes 786436
  158.0 2.0 copy-start.5
  163.8 53.1 %copy-start.7 = (bf16[2048,256]{1,0:T(8,128)(2,1)S(1)}, bf16[2048,256]{1,0:T(8,128)(2,1)}, u32[]{:S(2)}) copy-start(bf16[2048,256]{1,0:T(8,128)(2,1)} %param.21) | copy-start | bytes 3145732
  163.8 53.1 %copy-start.8 = (f32[256]{0:T(256)S(1)}, f32[256]{0:T(256)}, u32[]{:S(2)}) copy-start(f32[256]{0:T(256)} %param.14) | copy-start | bytes 3076
  163.8 89.4 %all-gather.5.cloned.1.call-start = ((), (), s32[]{:S(2)}) async-start(), calls=%async_computation.4 | async-start | bytes 3145728 | tf_op jit(solution)/shard_map/all_gather | solution.py:60
  216.9 3.1 copy-start.4
  253.3 7.6 %copy-start.6 = (bf16[4096,256]{1,0:T(8,128)(2,1)S(1)}, bf16[4096,256]{1,0:T(8,128)(2,1)}, u32[]{:S(2)}) copy-start(bf16[4096,256]{1,0:T(8,128)(2,1)} %all-gather.5.cloned.1.call-done) | copy-start | bytes 6291460
  253.3 84.1 %copy-start.1 = (bf16[1,102,128,128]{3,2,1,0:T(8,128)(2,1)S(1)}, bf16[1,102,128,128]{3,2,1,0:T(8,128)(2,1)}, u32[]{:S(2)}) copy-start(bf16[1,102,128,128]{3,2,1,0:T(8,128)(2,1)} %param.15) | copy-start | bytes 10027012
Sparse Core Ops, SparseCore 0:
  15.4 53.0 all-gather.2
  164.0 52.9 reduce-scatter.1
  220.1 33.1 all-gather.4
where the time goes:
time: 345 us; the launch traced here: 344 us
  waiting for transfers between devices  129 us (37%)
  blocking collectives  74.1 us (21%)
  local copies, waits for them, and re-layouts  62.7 us (18%)
  matrix products  41.8 us (12%)
  other arithmetic  14.5 us (4%)
  between operations  14.5 us (4%)
  starting transfers between devices  7.74 us (2%)
    psum x1, blocking collectives, body(): all_grads, bias_grad = lax.psum((all_grads, bias_grad), 'dom')  74.1 us
    reduce_scatter x1, waiting for transfers between devices, body(): lax.psum_scatter(jnp.dot(row_block, weights, preferred_element_type=jnp.f...  52.8 us
    all_gather x1, waiting for transfers between devices, body(): everyone = lax.all_gather(boundary, 'dom', axis=0, tiled=True)  39.3 us
    all_gather x1, waiting for transfers between devices, body(): shard_rows = lax.all_gather(pre_grad, 'feat', axis=0, tiled=True)  32.1 us
    dot_general x1, local copies, waits for them, and re-layouts, tile_sums(): jnp.einsum('etc,ecf->etf', local_tiles, picked, preferred_element_type=jn...  28.4 us
    dot_general x1, matrix products, tile_sums(): jnp.einsum('de,etf->dtf', onehot, products, precision=lax.Precision.HIGHEST)  16.6 us
    dot_general x1, matrix products, tile_sums(): jnp.einsum('etc,ecf->etf', local_tiles, picked, preferred_element_type=jn...  13.8 us
    gather x1, local copies, waits for them, and re-layouts, body(): received = jnp.take(everyone, wanted, axis=0)  12.2 us
  transfers between devices with their start and end apart: 4, of which 4 were waited for; matrix products, arithmetic and copies ran while one was open for 1% of the time, Pallas kernels for 0%

commit v1 on v0

--- a/solution.py
+++ b/solution.py
@@ -1,9 +1,35 @@
+import functools
 import jax
 import jax.numpy as jnp
 from jax import lax
 from jax.sharding import PartitionSpec as P
 
 TILE = 128
+
+
+def lay_the_slot(my_data, dev_axis):
+    local_now = lax.psum(1, axis_name=dev_axis)
+    r_now, response, met_up = (local_now, lax.axis_index(dev_axis), my_data.shape[0])
+    log = tuple((no * r_now if num == 0 else no for num, no in enumerate(my_data.shape)))
+    piece_now = jnp.zeros(log, my_data.dtype)
+    r1 = lax.dynamic_update_slice_in_dim(piece_now, my_data, response * met_up, axis=0)
+    vec_out = val = my_data
+    for dev_j in range(1, r_now // 2 + 1):
+        carry_in = tuple(((num, (num + 1) % r_now) for num in range(r_now)))
+        vec_out = lax.ppermute(vec_out, axis_name=dev_axis, perm=carry_in)
+        r1 = lax.dynamic_update_slice_in_dim(
+            r1, vec_out, (response - dev_j) % r_now * met_up, axis=0
+        )
+        if 2 * dev_j < r_now:
+            block_out = tuple(((num, (num - 1) % r_now) for num in range(r_now)))
+            val = lax.ppermute(val, axis_name=dev_axis, perm=block_out)
+            r1 = lax.dynamic_update_slice_in_dim(
+                r1, val, (response + dev_j) % r_now * met_up, axis=0
+            )
+    return r1
+
+
+shifts_all_trace = functools.partial(lay_the_slot, dev_axis="dom")
 
 
 def tile_sums(source, local_tiles, dest_list, source_list, live_count, dest_tiles):
@@ -36,7 +62,7 @@
     slice_width = features.shape[1]
     node_rows = features.shape[0]
     boundary = jnp.take(features, bound_rows[0], axis=0)
-    everyone = lax.all_gather(boundary, "dom", axis=0, tiled=True)
+    everyone = shifts_all_trace(boundary)
     pick_lists = lax.all_to_all(send_pick, "dom", split_axis=1, concat_axis=0, tiled=True)
     offsets = (jnp.arange(part_count, dtype=jnp.int32) * boundary.shape[0])[:, None]
     wanted = (pick_lists[:, 0, :] + offsets).reshape(-1)

time: 345 us -> 365 us (1.058)
  starting transfers between devices: 7.74 us -> 36.9 us
  waiting for transfers between devices: 129 us -> 103 us
  local copies, waits for them, and re-layouts: 62.7 us -> 80.5 us
    all_gather x1 -> x0, waiting for transfers between devices: 39.3 us -> none  [body(): everyone = lax.all_gather(boundary, 'dom', axis=0, tiled=True)]
    ppermute x0 -> x15, starting transfers between devices: none -> 32.9 us  [the longest x7 32.4 us: lay_the_slot(): val = lax.ppermute(val, axis_name=dev_axis, perm=block_out)]
    ppermute x0 -> x15, waiting for transfers between devices: none -> 18.9 us  [the longest x8 16 us: lay_the_slot(): vec_out = lax.ppermute(vec_out, axis_name=dev_axis, perm=carry_in)]
    dynamic_update_slice x0 -> x15, local copies, waits for them, and re-layouts: none -> 15.6 us  [the longest x8 8.63 us: lay_the_slot(): lax.dynamic_update_slice_in_dim(r1, vec_out, (response - dev_j) % r_now *...]
    all_to_all x1, waiting for transfers between devices: 4.32 us -> 0.01 us  [body(): lax.all_to_all(send_pick, 'dom', split_axis=1, concat_axis=0, tiled=True)]
    all_to_all x1, starting transfers between devices: 7.4 us -> 3.67 us  [body(): lax.all_to_all(send_pick, 'dom', split_axis=1, concat_axis=0, tiled=True)]
  transfers between devices with their start and end apart: 4 -> 18, of which waited for: 4 -> 13; matrix products, arithmetic and copies ran while one was open for 1% -> 4% of each run, Pallas kernels for 0% -> 0%
where the time goes in v1:
time: 365 us; the launch traced here: 364 us
  waiting for transfers between devices  103 us (28%)
  local copies, waits for them, and re-layouts  80.5 us (22%)
  blocking collectives  74.1 us (20%)
  matrix products  41.8 us (11%)
  starting transfers between devices  36.9 us (10%)
  between operations  15.2 us (4%)
  other arithmetic  12.4 us (3%)
    psum x1, blocking collectives, body(): all_grads, bias_grad = lax.psum((all_grads, bias_grad), 'dom')  74.1 us
    reduce_scatter x1, waiting for transfers between devices, body(): lax.psum_scatter(jnp.dot(row_block, weights, preferred_element_type=jnp.f...  52 us
    ppermute x7, starting transfers between devices, lay_the_slot(): val = lax.ppermute(val, axis_name=dev_axis, perm=block_out)  32.4 us
    all_gather x1, waiting for transfers between devices, body(): shard_rows = lax.all_gather(pre_grad, 'feat', axis=0, tiled=True)  32.1 us
    dot_general x1, local copies, waits for them, and re-layouts, tile_sums(): jnp.einsum('etc,ecf->etf', local_tiles, picked, preferred_element_type=jn...  28.4 us
    dot_general x1, matrix products, tile_sums(): jnp.einsum('de,etf->dtf', onehot, products, precision=lax.Precision.HIGHEST)  16.6 us
    ppermute x8, waiting for transfers between devices, lay_the_slot(): vec_out = lax.ppermute(vec_out, axis_name=dev_axis, perm=carry_in)  16 us
    dot_general x1, matrix products, tile_sums(): jnp.einsum('etc,ecf->etf', local_tiles, picked, preferred_element_type=jn...  13.8 us
  transfers between devices with their start and end apart: 18, of which 13 were waited for; matrix products, arithmetic and copies ran while one was open for 4% of the time, Pallas kernels for 0%

profile of v1, /device:TPU:0, one launch (start us, length us, event | category | flops | bytes accessed | tf_op | source)
XLA Modules:
  0.0 363.9 jit_solution(17713927793604850750)
XLA Ops:
  8.9 4.6 %gather_fusion = bf16[256,512]{1,0:T(8,128)(2,1)} fusion(bf16[4096,512]{1,0:T(8,128)(2,1)} %param.11, s32[1024]{0:T(1024)S(1)} %pad_clamp_fusion.1), kind=kCustom, calls=%fused_computation | custom fusion | bytes 525312 | tf_op jit(solution)/shard_map/jit(_take)/gather | solution.py:64
  17.2 4.9 %collective-permute-start.1 = (bf16[256,512]{1,0:T(8,128)(2,1)}, bf16[256,512]{1,0:T(8,128)(2,1)}, u32[]{:S(2)}, u32[]{:S(2)}) collective-permute-start(bf16[256,512]{1,0:T(8,128)(2,1)} %get-tuple-element.7), channel_id=1, source_target_pairs={{0,30},{2,0},{4,2},{6,4},{8,6},{10,8},{12,10},{14,12},{16,14},{18,... | collective-permute-start | bytes 786440 | tf_op jit(solution)/shard_map/ppermute | solution.py:25
  22.1 3.7 %all-to-all-start = ((s32[1,16,128]{2,0,1:T(1,128)}), s32[1,16,128]{2,0,1:T(1,128)S(1)}, u32[]{:S(2)}, u32[]{:S(2)}) async-start(s32[1,16,128]{2,0,1:T(1,128)} %bitcast.4), calls=%async_computation | async-start | bytes 16384 | tf_op jit(solution)/shard_map/all_to_all | solution.py:66
  27.6 4.5 %collective-permute-start.3 = (bf16[256,512]{1,0:T(8,128)(2,1)}, bf16[256,512]{1,0:T(8,128)(2,1)}, u32[]{:S(2)}, u32[]{:S(2)}) collective-permute-start(bf16[256,512]{1,0:T(8,128)(2,1)} %collective-permute-done.1), channel_id=1, source_target_pairs={{0,30},{2,0},{4,2},{6,4},{8,6},{10,8},{12,10},{14,12},{16,14},{18,... | collective-permute-start | bytes 786440 | tf_op jit(solution)/shard_map/ppermute | solution.py:25
  32.1 3.5 collective-permute-done.2
  36.3 4.7 %collective-permute-start.5 = (bf16[256,512]{1,0:T(8,128)(2,1)}, bf16[256,512]{1,0:T(8,128)(2,1)S(1)}, u32[]{:S(2)}, u32[]{:S(2)}) collective-permute-start(bf16[256,512]{1,0:T(8,128)(2,1)} %collective-permute-done.3), channel_id=1, source_target_pairs={{0,30},{2,0},{4,2},{6,4},{8,6},{10,8},{12,10},{14,12},{16,14},{18,... | collective-permute-start | bytes 786440 | tf_op jit(solution)/shard_map/ppermute | solution.py:25
  41.0 3.5 collective-permute-done.4
  46.2 4.4 %collective-permute-start.7 = (bf16[256,512]{1,0:T(8,128)(2,1)S(1)}, bf16[256,512]{1,0:T(8,128)(2,1)S(1)}, u32[]{:S(2)}, u32[]{:S(2)}) collective-permute-start(bf16[256,512]{1,0:T(8,128)(2,1)S(1)} %collective-permute-done.5), channel_id=1, source_target_pairs={{0,30},{2,0},{4,2},{6,4},{8,6},{10,8},{12,10},{14,12},{16,14},{18,... | collective-permute-start | bytes 786440 | tf_op jit(solution)/shard_map/ppermute | solution.py:25
  56.6 4.5 %collective-permute-start.9 = (bf16[256,512]{1,0:T(8,128)(2,1)S(1)}, bf16[256,512]{1,0:T(8,128)(2,1)S(1)}, u32[]{:S(2)}, u32[]{:S(2)}) collective-permute-start(bf16[256,512]{1,0:T(8,128)(2,1)S(1)} %collective-permute-done.7), channel_id=1, source_target_pairs={{0,30},{2,0},{4,2},{6,4},{8,6},{10,8},{12,10},{14,12},{16,14},{18,... | collective-permute-start | bytes 786440 | tf_op jit(solution)/shard_map/ppermute | solution.py:25
  64.9 4.7 %collective-permute-start.11 = (bf16[256,512]{1,0:T(8,128)(2,1)S(1)}, bf16[256,512]{1,0:T(8,128)(2,1)S(1)}, u32[]{:S(2)}, u32[]{:S(2)}) collective-permute-start(bf16[256,512]{1,0:T(8,128)(2,1)S(1)} %collective-permute-done.9), channel_id=1, source_target_pairs={{0,30},{2,0},{4,2},{6,4},{8,6},{10,8},{12,10},{14,12},{16,14},{18,... | collective-permute-start | bytes 786440 | tf_op jit(solution)/shard_map/ppermute | solution.py:25
  73.5 4.7 %collective-permute-start.13 = (bf16[256,512]{1,0:T(8,128)(2,1)S(1)}, bf16[256,512]{1,0:T(8,128)(2,1)S(1)}, u32[]{:S(2)}, u32[]{:S(2)}) collective-permute-start(bf16[256,512]{1,0:T(8,128)(2,1)S(1)} %collective-permute-done.11), channel_id=1, source_target_pairs={{0,30},{2,0},{4,2},{6,4},{8,6},{10,8},{12,10},{14,12},{16,14},{18,... | collective-permute-start | bytes 786440 | tf_op jit(solution)/shard_map/ppermute | solution.py:25
  82.8 5.6 %collective-permute-done.14 = bf16[256,512]{1,0:T(8,128)(2,1)S(1)} collective-permute-done((bf16[256,512]{1,0:T(8,128)(2,1)S(1)}, bf16[256,512]{1,0:T(8,128)(2,1)S(1)}, u32[]{:S(2)}, u32[]{:S(2)}) %collective-permute-start.14) | collective-permute-done | bytes 262176 | tf_op jit(solution)/shard_map/ppermute | solution.py:19
  89.1 12.2 %gather_fusion.1 = bf16[2048,512]{1,0:T(8,128)(2,1)} fusion(bf16[4096,512]{1,0:T(8,128)(2,1)} %constant_dynamic-update-slice_fusion, s32[2048]{0:T(1024)S(1)} %broadcast_clamp_fusion), kind=kCustom, calls=%fused_computation.1 | custom fusion | bytes 4202496 | tf_op jit(solution)/shard_map/jit(_take)/gather | solution.py:69
  104.1 3.0 pad_maximum_fusion.1
  107.1 10.2 %gather_fusion.2 = bf16[102,128,512]{2,1,0:T(8,128)(2,1)} fusion(bf16[48,128,512]{2,1,0:T(8,128)(2,1)} %bitcast.39, s32[1024]{0:T(1024)S(1)} %pad_clamp_fusion), kind=kCustom, calls=%fused_computation.2 | custom fusion | bytes 26739096 | tf_op jit(solution)/shard_map/jit(_take)/gather | solution.py:38
  117.3 13.8 %fusion.3 = f32[102,128,512]{1,2,0:T(8,128)} fusion(bf16[102,128,512]{2,1,0:T(8,128)(2,1)} %gather_fusion.2, pred[102]{0:T(512)(128)(4,1)S(1)} %compare_and_fusion.2, bf16[1,102,128,128]{3,2,1,0:T(8,128)(2,1)S(1)} %copy-done), kind=kOutput, calls=%fused_computation.6 | convolution fusion | flops 1717960704 | bytes 43450472 | tf_op jit(solution)/shard_map/etc,ecf->etf/dot_general | solution.py:39
  131.1 28.4 %copy.21 = f32[102,128,512]{2,0,1:T(8,128)} copy(f32[102,128,512]{1,2,0:T(8,128)} %fusion.3) | data formatting | bytes 53477376 | tf_op jit(solution)/shard_map/etc,ecf->etf/dot_general | solution.py:39
  159.5 16.6 %convolution_convert_fusion = bf16[32,128,512]{2,0,1:T(8,128)(2,1)S(1)} fusion(f32[102,128,512]{2,0,1:T(8,128)} %copy.21, f32[102]{0:T(128)S(1)} %compare_convert_fusion, s32[102]{0:T(128)S(1)} %bitcast.47), kind=kOutput, calls=%fused_computation.14 | convolution fusion | flops 2569017856 | bytes 30933808 | tf_op jit(solution)/shard_map/de,etf->dtf/dot_general | solution.py:44
  180.5 3.9 %fusion.8 = f32[4096,256]{1,0:T(8,128)} fusion(bf16[4096,512]{1,0:T(8,128)(2,1)S(1)} %bitcast.40, bf16[4096,512]{1,0:T(8,128)(2,1)S(1)} %copy-done.3, bf16[512,256]{1,0:T(8,128)(2,1)S(1)} %copy-done.11, bf16[512,256]{1,0:T(8,128)(2,1)S(1)} %copy-done.12), kind=kOutput, calls=%fused_computation.11 | convolution fusion | flops 2165309440 | bytes 13107200 | tf_op jit(solution)/shard_map/dot_general | solution.py:78
  184.7 52.0 %reduce-scatter.2.cloned.1.call-done = f32[2048,256]{1,0:T(8,128)} async-done(((f32[4096,256]{1,0:T(8,128)}), f32[2048,256]{1,0:T(8,128)}) %reduce-scatter.2.cloned.1.call-update) | async-done | bytes 2097168 | tf_op jit(solution)/shard_map/reduce_scatter | solution.py:77
  236.7 3.0 compare_select_fusion
  240.9 32.1 %all-gather.2.cloned.1.call-done = bf16[4096,256]{1,0:T(8,128)(2,1)} async-done(((bf16[2048,256]{1,0:T(8,128)(2,1)}), bf16[4096,256]{1,0:T(8,128)(2,1)}) %all-gather.2.cloned.1.call-update) | async-done | bytes 2097168 | tf_op jit(solution)/shard_map/all_gather | solution.py:86
  273.0 7.5 %fusion.7 = f32[1024,256]{1,0:T(8,128)} fusion(bf16[4096,256]{1,0:T(8,128)(2,1)} %all-gather.2.cloned.1.call-done, bf16[4096,512]{1,0:T(8,128)(2,1)} %bitcast.41, bf16[4096,512]{1,0:T(8,128)(2,1)} %param.11), kind=kOutput, calls=%fused_computation.10 | convolution fusion | flops 2164260864 | bytes 11534336 | tf_op jit(solution)/shard_map/dot_general | solution.py:88
  281.1 74.1 %all-reduce.2 = (bf16[1024,256]{1,0:T(8,128)(2,1)}, f32[256]{0:T(256)}) all-reduce(f32[1024,256]{1,0:T(8,128)} %fusion.7, f32[256]{0:T(256)S(1)} %convert_reduce_fusion), channel_id=1, replica_groups=mesh['dom'=16,'feat'=2] {'dom'}, use_global_device_ids=true, to_apply=%region_1.2 | all-reduce | flops 262400 | bytes 1574912 | tf_op jit(solution)/shard_map/psum | solution.py:93
  (87 shorter events, 38.8 us)
Async XLA Ops:
  7.2 110.1 %copy-start = (bf16[1,102,128,128]{3,2,1,0:T(8,128)(2,1)S(1)}, bf16[1,102,128,128]{3,2,1,0:T(8,128)(2,1)}, u32[]{:S(2)}) copy-start(bf16[1,102,128,128]{3,2,1,0:T(8,128)(2,1)} %param.15) | copy-start | bytes 10027012
  7.2 18.7 %copy-start.13 = (s32[1,102]{1,0:T(1,128)S(1)}, s32[1,102]{1,0:T(1,128)}, u32[]{:S(2)}) copy-start(s32[1,102]{1,0:T(1,128)} %param.17) | copy-start | bytes 1228
  16.7 9.9 %collective-permute-start = (bf16[256,512]{1,0:T(8,128)(2,1)}, bf16[256,512]{1,0:T(8,128)(2,1)}, u32[]{:S(2)}, u32[]{:S(2)}) collective-permute-start(bf16[256,512]{1,0:T(8,128)(2,1)} %get-tuple-element.7), channel_id=1, source_target_pairs={{0,2},{2,4},{4,6},{6,8},{8,10},{10,12},{12,14},{14,16},{16,18},{18... | collective-permute-start | bytes 786440 | tf_op jit(solution)/shard_map/ppermute | solution.py:19
  17.2 10.4 %collective-permute-start.1 = (bf16[256,512]{1,0:T(8,128)(2,1)}, bf16[256,512]{1,0:T(8,128)(2,1)}, u32[]{:S(2)}, u32[]{:S(2)}) collective-permute-start(bf16[256,512]{1,0:T(8,128)(2,1)} %get-tuple-element.7), channel_id=1, source_target_pairs={{0,30},{2,0},{4,2},{6,4},{8,6},{10,8},{12,10},{14,12},{16,14},{18,... | collective-permute-start | bytes 786440 | tf_op jit(solution)/shard_map/ppermute | solution.py:25
  22.1 13.4 %all-to-all-start = ((s32[1,16,128]{2,0,1:T(1,128)}), s32[1,16,128]{2,0,1:T(1,128)S(1)}, u32[]{:S(2)}, u32[]{:S(2)}) async-start(s32[1,16,128]{2,0,1:T(1,128)} %bitcast.4), calls=%async_computation | async-start | bytes 16384 | tf_op jit(solution)/shard_map/all_to_all | solution.py:66
  25.8 210.9 %reduce-scatter.2.cloned.1.call-start = ((), (), s32[]{:S(2)}) async-start(), calls=%async_computation.2 | async-start | bytes 6291456 | tf_op jit(solution)/shard_map/reduce_scatter | solution.py:77
  26.6 8.9 %collective-permute-start.2 = (bf16[256,512]{1,0:T(8,128)(2,1)}, bf16[256,512]{1,0:T(8,128)(2,1)}, u32[]{:S(2)}, u32[]{:S(2)}) collective-permute-start(bf16[256,512]{1,0:T(8,128)(2,1)} %collective-permute-done), channel_id=1, source_target_pairs={{0,2},{2,4},{4,6},{6,8},{8,10},{10,12},{12,14},{14,16},{16,18},{18... | collective-permute-start | bytes 786440 | tf_op jit(solution)/shard_map/ppermute | solution.py:19
  27.6 8.7 %collective-permute-start.3 = (bf16[256,512]{1,0:T(8,128)(2,1)}, bf16[256,512]{1,0:T(8,128)(2,1)}, u32[]{:S(2)}, u32[]{:S(2)}) collective-permute-start(bf16[256,512]{1,0:T(8,128)(2,1)} %collective-permute-done.1), channel_id=1, source_target_pairs={{0,30},{2,0},{4,2},{6,4},{8,6},{10,8},{12,10},{14,12},{16,14},{18,... | collective-permute-start | bytes 786440 | tf_op jit(solution)/shard_map/ppermute | solution.py:25
  35.5 8.9 %collective-permute-start.4 = (bf16[256,512]{1,0:T(8,128)(2,1)}, bf16[256,512]{1,0:T(8,128)(2,1)}, u32[]{:S(2)}, u32[]{:S(2)}) collective-permute-start(bf16[256,512]{1,0:T(8,128)(2,1)} %collective-permute-done.2), channel_id=1, source_target_pairs={{0,2},{2,4},{4,6},{6,8},{8,10},{10,12},{12,14},{14,16},{16,18},{18... | collective-permute-start | bytes 786440 | tf_op jit(solution)/shard_map/ppermute | solution.py:19
  36.3 9.9 %collective-permute-start.5 = (bf16[256,512]{1,0:T(8,128)(2,1)}, bf16[256,512]{1,0:T(8,128)(2,1)S(1)}, u32[]{:S(2)}, u32[]{:S(2)}) collective-permute-start(bf16[256,512]{1,0:T(8,128)(2,1)} %collective-permute-done.3), channel_id=1, source_target_pairs={{0,30},{2,0},{4,2},{6,4},{8,6},{10,8},{12,10},{14,12},{16,14},{18,... | collective-permute-start | bytes 786440 | tf_op jit(solution)/shard_map/ppermute | solution.py:25
  44.4 8.8 %collective-permute-start.6 = (bf16[256,512]{1,0:T(8,128)(2,1)}, bf16[256,512]{1,0:T(8,128)(2,1)S(1)}, u32[]{:S(2)}, u32[]{:S(2)}) collective-permute-start(bf16[256,512]{1,0:T(8,128)(2,1)} %collective-permute-done.4), channel_id=1, source_target_pairs={{0,2},{2,4},{4,6},{6,8},{8,10},{10,12},{12,14},{14,16},{16,18},{18... | collective-permute-start | bytes 786440 | tf_op jit(solution)/shard_map/ppermute | solution.py:19
  46.2 10.4 %collective-permute-start.7 = (bf16[256,512]{1,0:T(8,128)(2,1)S(1)}, bf16[256,512]{1,0:T(8,128)(2,1)S(1)}, u32[]{:S(2)}, u32[]{:S(2)}) collective-permute-start(bf16[256,512]{1,0:T(8,128)(2,1)S(1)} %collective-permute-done.5), channel_id=1, source_target_pairs={{0,30},{2,0},{4,2},{6,4},{8,6},{10,8},{12,10},{14,12},{16,14},{18,... | collective-permute-start | bytes 786440 | tf_op jit(solution)/shard_map/ppermute | solution.py:25
  53.2 9.5 %collective-permute-start.8 = (bf16[256,512]{1,0:T(8,128)(2,1)S(1)}, bf16[256,512]{1,0:T(8,128)(2,1)S(1)}, u32[]{:S(2)}, u32[]{:S(2)}) collective-permute-start(bf16[256,512]{1,0:T(8,128)(2,1)S(1)} %collective-permute-done.6), channel_id=1, source_target_pairs={{0,2},{2,4},{4,6},{6,8},{8,10},{10,12},{12,14},{14,16},{16,18},{18... | collective-permute-start | bytes 786440 | tf_op jit(solution)/shard_map/ppermute | solution.py:19
  56.6 8.3 %collective-permute-start.9 = (bf16[256,512]{1,0:T(8,128)(2,1)S(1)}, bf16[256,512]{1,0:T(8,128)(2,1)S(1)}, u32[]{:S(2)}, u32[]{:S(2)}) collective-permute-start(bf16[256,512]{1,0:T(8,128)(2,1)S(1)} %collective-permute-done.7), channel_id=1, source_target_pairs={{0,30},{2,0},{4,2},{6,4},{8,6},{10,8},{12,10},{14,12},{16,14},{18,... | collective-permute-start | bytes 786440 | tf_op jit(solution)/shard_map/ppermute | solution.py:25
  62.7 8.6 %collective-permute-start.10 = (bf16[256,512]{1,0:T(8,128)(2,1)S(1)}, bf16[256,512]{1,0:T(8,128)(2,1)S(1)}, u32[]{:S(2)}, u32[]{:S(2)}) collective-permute-start(bf16[256,512]{1,0:T(8,128)(2,1)S(1)} %collective-permute-done.8), channel_id=1, source_target_pairs={{0,2},{2,4},{4,6},{6,8},{8,10},{10,12},{12,14},{14,16},{16,18},{18... | collective-permute-start | bytes 786440 | tf_op jit(solution)/shard_map/ppermute | solution.py:19
  64.9 8.6 %collective-permute-start.11 = (bf16[256,512]{1,0:T(8,128)(2,1)S(1)}, bf16[256,512]{1,0:T(8,128)(2,1)S(1)}, u32[]{:S(2)}, u32[]{:S(2)}) collective-permute-start(bf16[256,512]{1,0:T(8,128)(2,1)S(1)} %collective-permute-done.9), channel_id=1, source_target_pairs={{0,30},{2,0},{4,2},{6,4},{8,6},{10,8},{12,10},{14,12},{16,14},{18,... | collective-permute-start | bytes 786440 | tf_op jit(solution)/shard_map/ppermute | solution.py:25
  71.3 8.6 %collective-permute-start.12 = (bf16[256,512]{1,0:T(8,128)(2,1)S(1)}, bf16[256,512]{1,0:T(8,128)(2,1)S(1)}, u32[]{:S(2)}, u32[]{:S(2)}) collective-permute-start(bf16[256,512]{1,0:T(8,128)(2,1)S(1)} %collective-permute-done.10), channel_id=1, source_target_pairs={{0,2},{2,4},{4,6},{6,8},{8,10},{10,12},{12,14},{14,16},{16,18},{18... | collective-permute-start | bytes 786440 | tf_op jit(solution)/shard_map/ppermute | solution.py:19
  73.5 8.6 %collective-permute-start.13 = (bf16[256,512]{1,0:T(8,128)(2,1)S(1)}, bf16[256,512]{1,0:T(8,128)(2,1)S(1)}, u32[]{:S(2)}, u32[]{:S(2)}) collective-permute-start(bf16[256,512]{1,0:T(8,128)(2,1)S(1)} %collective-permute-done.11), channel_id=1, source_target_pairs={{0,30},{2,0},{4,2},{6,4},{8,6},{10,8},{12,10},{14,12},{16,14},{18,... | collective-permute-start | bytes 786440 | tf_op jit(solution)/shard_map/ppermute | solution.py:25
  79.9 8.5 %collective-permute-start.14 = (bf16[256,512]{1,0:T(8,128)(2,1)S(1)}, bf16[256,512]{1,0:T(8,128)(2,1)S(1)}, u32[]{:S(2)}, u32[]{:S(2)}) collective-permute-start(bf16[256,512]{1,0:T(8,128)(2,1)S(1)} %collective-permute-done.12), channel_id=1, source_target_pairs={{0,2},{2,4},{4,6},{6,8},{8,10},{10,12},{12,14},{14,16},{16,18},{18... | collective-permute-start | bytes 786440 | tf_op jit(solution)/shard_map/ppermute | solution.py:19
  131.1 28.4 %copy-start.10 = (s32[1,102]{1,0:T(1,128)S(1)}, s32[1,102]{1,0:T(1,128)}, u32[]{:S(2)}) copy-start(s32[1,102]{1,0:T(1,128)} %param.16) | copy-start | bytes 1228
  184.4 52.3 %copy-start.7 = (bf16[2048,256]{1,0:T(8,128)(2,1)S(1)}, bf16[2048,256]{1,0:T(8,128)(2,1)}, u32[]{:S(2)}) copy-start(bf16[2048,256]{1,0:T(8,128)(2,1)} %param.21) | copy-start | bytes 3145732
  184.4 52.3 %copy-start.9 = (f32[256]{0:T(256)S(1)}, f32[256]{0:T(256)}, u32[]{:S(2)}) copy-start(f32[256]{0:T(256)} %param.14) | copy-start | bytes 3076
  184.4 88.6 %all-gather.2.cloned.1.call-start = ((), (), s32[]{:S(2)}) async-start(), calls=%async_computation.3 | async-start | bytes 3145728 | tf_op jit(solution)/shard_map/all_gather | solution.py:86
  273.0 84.1 %copy-start.1 = (bf16[1,102,128,128]{3,2,1,0:T(8,128)(2,1)S(1)}, bf16[1,102,128,128]{3,2,1,0:T(8,128)(2,1)}, u32[]{:S(2)}) copy-start(bf16[1,102,128,128]{3,2,1,0:T(8,128)(2,1)} %param.15) | copy-start | bytes 10027012
  (8 other events, 30.8 us)
Sparse Core Ops, SparseCore 0:
  184.5 52.1 reduce-scatter.1
  239.9 33.0 all-gather.1
